TPU v7x, 32 devices: a whole 2x2x4 slice. The times are simulated.
32 devices in a mesh: wide: 8 (over z, x), narrow: 4 (over y, core).
Axes of the slice: x: 2, y: 2, z: 4, core: 2. Of those that a mesh axis runs over, the one named last changes fastest.
Arguments:
- star_pos: float32 [3, 2048], P(None, ('wide', 'narrow')), may hold values from -6 to 6
- star_vel: float32 [3, 2048], P(None, ('wide', 'narrow')), may hold values from -6 to 6
- star_mass: float32 [2048], P(('wide', 'narrow')), may hold values from 0.00048828125 to 0.0048828125
- star_acc: float32 [3, 2048], P(None, ('wide', 'narrow')), may hold values from -6 to 6
- star_jerk: float32 [3, 2048], P(None, ('wide', 'narrow')), may hold values from -120 to 120
- gal_pos: float32 [3, 16384], P(None, ('wide', 'narrow')), may hold values from -6 to 6
- gal_vel: float32 [3, 16384], P(None, ('wide', 'narrow')), may hold values from -6 to 6
- gal_mass: float32 [16384], P(('wide', 'narrow')), may hold values from 0.0009765625 to 0.009765625
- group_of: int32 [16384], P(('wide', 'narrow')), may hold values from 0 to 31, as said below
- let_send: int32 [32, 8, 1], P(('wide', 'narrow')), may hold values from -1 to 3, as said below
- star_leaf: int32 [128, 8], P(('wide', 'narrow')), may hold values from 0 to 7, as said below
Outputs:
- gal_vel_new: float32 [3, 16384], P(None, ('wide', 'narrow'))
- star_pos_new: float32 [3, 2048], P(None, ('wide', 'narrow'))
- star_vel_new: float32 [3, 2048], P(None, ('wide', 'narrow'))
Inputs may be any that keep to these rules, and one draw needn't show every extreme that they name: `group_of`: within each leaf of 128 bodies every group number is held by exactly 4 bodies. `let_send`: entry [k, j, s] is a local leaf of device k sent to the device of wide index j with k's narrow index, or -1 for an empty slot; the leaves of one row are distinct; a device lists nothing for its own wide index; for some wide index j, every device whose wide index is not j lists a leaf for j, in every draw. `star_leaf`: the star blocks listed for one leaf are distinct.
All inputs are finite; a program needn't handle non-finite values.
Results may differ from a plain program's by a relative error of at most 0.0003.
Values sent between devices are 32-bit elements; how exact they have to be, the bound alone decides.
A program may use at most 64 MiB of HBM per device.

v0:
```python
import math

import jax
import jax.numpy as jnp
from jax import lax
from jax.sharding import PartitionSpec as P

GROUPS = 32


time_step = 0.25
soften_sq = 0.05


def by_blocks(kernel, arrays):
    total_rows = arrays[0].shape[1]
    block_rows = math.gcd(total_rows, 512)
    nblocks = total_rows // block_rows
    split = tuple(
        (
            member.reshape(member.shape[0], nblocks, block_rows).transpose(1, 0, 2)
            for member in arrays
        )
    )
    result = lax.map(kernel, split)
    return jax.tree.map(
        lambda piece: piece.transpose(1, 0, 2).reshape(piece.shape[1], total_rows), result
    )


def attract(tgt_pos, src_pos, src_mass):

    def kernel(pieces):
        here_pos = pieces[0]
        offset = src_pos[:, None, :] - here_pos[:, :, None]
        dist_sq = jnp.sum(offset * offset, axis=0) + soften_sq
        inverse = lax.rsqrt(dist_sq)
        weight = src_mass[None, :] * inverse * inverse * inverse
        return jnp.sum(offset * weight[None], axis=2)

    return by_blocks(kernel, (tgt_pos,))


def hermite(tgt_pos, tgt_vel, src_pos, src_vel, src_mass):

    def kernel(pieces):
        here_pos, here_vel = pieces
        offset = src_pos[:, None, :] - here_pos[:, :, None]
        rel_vel = src_vel[:, None, :] - here_vel[:, :, None]
        dist_sq = jnp.sum(offset * offset, axis=0) + soften_sq
        inverse = lax.rsqrt(dist_sq)
        weight = src_mass[None, :] * inverse * inverse * inverse
        approach = 3.0 * jnp.sum(offset * rel_vel, axis=0) / dist_sq
        accel_sum = jnp.sum(offset * weight[None], axis=2)
        jerk_sum = jnp.sum((rel_vel - offset * approach[None]) * weight[None], axis=2)
        return (accel_sum, jerk_sum)

    return by_blocks(kernel, (tgt_pos, tgt_vel))


def body(
    star_pos,
    star_vel,
    star_mass,
    star_acc,
    star_jerk,
    gal_pos,
    gal_vel,
    gal_mass,
    group_of,
    let_send,
    star_leaf,
):
    n_wide = lax.axis_size("wide")
    own_count = star_pos.shape[1]
    leaves = star_leaf.shape[0]
    leaf_size = gal_pos.shape[1] // leaves
    groups_per = GROUPS
    step_sq = time_step * time_step
    pred_pos = (
        star_pos
        + time_step * star_vel
        + step_sq * 0.5 * star_acc
        + step_sq * time_step / 6.0 * star_jerk
    )
    pred_vel = star_vel + time_step * star_acc + step_sq * 0.5 * star_jerk
    own_state = jnp.concatenate([pred_pos, pred_vel, star_mass[None]], axis=0)
    sibling = lax.all_gather(own_state, "narrow", axis=1, tiled=True)
    columns = lax.all_gather(own_state, "wide", axis=1, tiled=True)
    onehot = (
        group_of.reshape(leaves, 1, leaf_size)
        == jnp.arange(groups_per, dtype=jnp.int32)[None, :, None]
    ).astype(jnp.float32)
    leaf_mass = gal_mass.reshape(leaves, leaf_size)
    leaf_pos = gal_pos.reshape(3, leaves, leaf_size)
    cell_mass = jnp.einsum("lgb,lb->lg", onehot, leaf_mass, precision=lax.Precision.HIGHEST)
    cell_mom = jnp.einsum(
        "lgb,clb->clg", onehot, leaf_pos * leaf_mass[None], precision=lax.Precision.HIGHEST
    )
    cells = jnp.concatenate([cell_mom / cell_mass[None], cell_mass[None]], axis=0)
    slot_ids = let_send[0]
    chosen = (slot_ids[:, :, None] == jnp.arange(leaves, dtype=jnp.int32)[None, None, :]).astype(
        jnp.float32
    )
    outgoing = jnp.einsum("wsl,clg->wcsg", chosen, cells, precision=lax.Precision.HIGHEST)
    outgoing = outgoing.reshape(n_wide, 4, slot_ids.shape[1] * groups_per)
    received = lax.all_to_all(outgoing, "wide", split_axis=0, concat_axis=0, tiled=True)
    essential = received.transpose(1, 0, 2).reshape(4, -1)
    local_cells = cells.reshape(4, leaves * groups_per)
    accel_part, jerk_part = hermite(
        sibling[0:3], sibling[3:6], columns[0:3], columns[3:6], columns[6]
    )
    summed = lax.psum_scatter(
        jnp.concatenate([accel_part, jerk_part], axis=0), "narrow", scatter_dimension=1, tiled=True
    )
    gal_acc = attract(gal_pos, gal_pos, gal_mass) + attract(gal_pos, essential[0:3], essential[3])
    picked = jnp.take(columns.reshape(7, n_wide, own_count), star_leaf, axis=1)
    picked = picked.reshape(7, leaves, star_leaf.shape[1] * own_count)
    star_term = jax.vmap(
        lambda target, source: attract(target, source[0:3], source[6]), in_axes=(1, 1), out_axes=1
    )(leaf_pos, picked)
    gal_acc = gal_acc + star_term.reshape(3, leaves * leaf_size)
    gal_vel_new = gal_vel + time_step * gal_acc
    all_cells = jnp.concatenate([local_cells, essential], axis=1)
    cell_acc = attract(pred_pos, all_cells[0:3], all_cells[3])
    new_acc = summed[0:3] + cell_acc
    new_jerk = summed[3:6]
    star_vel_new = (
        star_vel + time_step * 0.5 * (star_acc + new_acc) + step_sq / 12.0 * (star_jerk - new_jerk)
    )
    star_pos_new = (
        star_pos
        + time_step * 0.5 * (star_vel + star_vel_new)
        + step_sq / 12.0 * (star_acc - new_acc)
    )
    return (gal_vel_new, star_pos_new, star_vel_new)


def solution(mesh):
    placed = (
        P(None, ("wide", "narrow")),
        P(None, ("wide", "narrow")),
        P(("wide", "narrow")),
        P(None, ("wide", "narrow")),
        P(None, ("wide", "narrow")),
        P(None, ("wide", "narrow")),
        P(None, ("wide", "narrow")),
        P(("wide", "narrow")),
        P(("wide", "narrow")),
        P(("wide", "narrow"), None, None),
        P(("wide", "narrow"), None),
    )
    return jax.shard_map(
        body,
        mesh=mesh,
        in_specs=placed,
        out_specs=(
            P(None, ("wide", "narrow")),
            P(None, ("wide", "narrow")),
            P(None, ("wide", "narrow")),
        ),
        check_vma=False,
    )
```

profile of v0, /device:TPU:0, one launch (start us, length us, event | category | flops | bytes accessed | tf_op | source)
XLA Modules:
  0.0 87.1 jit_solution(16347241939596092432)
XLA Ops:
  7.2 0.8 fusion.15
  8.0 0.9 %fusion.11 = f32[3,4,32]{2,0,1:T(4,128)S(1)} fusion(s32[4,128]{1,0:T(4,128)} %bitcast.83, f32[3,512]{1,0:T(4,128)} %param.16, f32[4,32]{1,0:T(4,128)S(1)} %bitcast.76, f32[4,128]{1,0:T(4,128)} %bitcast.80), kind=kOutput, calls=%fused_computation.27 | convolution fusion | flops 608128 | bytes 12288 | tf_op jit(solution)/shard_map/lgb,clb->clg/dot_general | solution.py:97
  8.9 0.8 convolution_bitcast_fusion
  9.8 0.7 reshape.231
  10.5 7.3 %all-to-all-start = ((f32[8,1,128]{2,1,0:T(1,128)}), f32[8,1,128]{2,1,0:T(1,128)S(1)}, u32[]{:S(2)}, u32[]{:S(2)}) async-start(f32[8,1,128]{2,1,0:T(1,128)} %reshape.231), calls=%async_computation | async-start | bytes 8192 | tf_op jit(solution)/shard_map/all_to_all | solution.py:107
  17.8 0.7 multiply_add_fusion.3
  18.5 0.7 maximum_bitcast_fusion
  19.2 5.2 %all-gather.1 = f32[4,64,7]{1,2,0:T(8,128)S(1)} all-gather(f32[1,64,7]{1,2,0:T(8,128)S(1)} %maximum_bitcast_fusion), channel_id=1, replica_groups=mesh['wide'=8,'narrow'=4] {'narrow'}, dimensions={0}, use_global_device_ids=true | all-gather | bytes 8960 | tf_op jit(solution)/shard_map/all_gather | solution.py:88
  24.4 31.1 %all-gather = f32[8,64,7]{1,2,0:T(8,128)S(1)} all-gather(f32[1,64,7]{1,2,0:T(8,128)S(1)} %maximum_bitcast_fusion), channel_id=1, replica_groups=mesh['wide'=8,'narrow'=4] {'wide'}, dimensions={0}, use_global_device_ids=true | all-gather | bytes 16128 | tf_op jit(solution)/shard_map/all_gather | solution.py:89
  55.7 0.4 fusion.8
  56.3 0.8 fusion.9
  57.0 0.8 copy.79
  58.1 0.6 gather_fusion
  58.8 0.4 fusion
  59.3 0.4 fusion.2
  59.9 0.7 fusion.3
  60.8 0.6 fusion.1
  61.6 0.5 broadcast.179
  62.1 0.7 reduce.6
  63.7 0.5 fusion.5
  64.2 0.6 fusion.19
  65.0 13.5 %reduce-scatter.4.cloned.1.call-done = f32[64,6]{1,0:T(8,128)} async-done(((f32[256,6]{1,0:T(8,128)}), f32[64,6]{1,0:T(8,128)}) %reduce-scatter.4.cloned.1.call-update) | async-done | bytes 1552
  78.6 0.9 %fusion.25 = (f32[3,64]{0,1:T(8,128)S(1)}, f32[3,64]{0,1:T(8,128)S(1)}) fusion(f32[6,64]{0,1:T(8,128)} %bitcast.69), kind=kLoop, calls=%fused_computation.64 | loop fusion | bytes 3072 | tf_op jit(solution)/shard_map/slice | solution.py:127
  79.7 0.6 multiply_add_fusion
  (65 shorter events, 2.7 us)
Async XLA Ops:
  10.5 51.1 %all-to-all-start = ((f32[8,1,128]{2,1,0:T(1,128)}), f32[8,1,128]{2,1,0:T(1,128)S(1)}, u32[]{:S(2)}, u32[]{:S(2)}) async-start(f32[8,1,128]{2,1,0:T(1,128)} %reshape.231), calls=%async_computation | async-start | bytes 8192 | tf_op jit(solution)/shard_map/all_to_all | solution.py:107
  17.8 60.8 %reduce-scatter.4.cloned.1.call-start = ((), (), s32[]{:S(2)}) async-start(), calls=%async_computation.2 | async-start | bytes 163840
  56.2 1.6 %copy-start.2 = (s32[4,8]{1,0:T(4,128)S(1)}, s32[4,8]{1,0:T(4,128)}, u32[]{:S(2)}) copy-start(s32[4,8]{1,0:T(4,128)} %param.21) | copy-start | bytes 388
  56.2 1.6 %copy-start = (f32[3,512]{1,0:T(4,128)S(1)}, f32[3,512]{1,0:T(4,128)}, u32[]{:S(2)}) copy-start(f32[3,512]{1,0:T(4,128)} %param.16) | copy-start | bytes 18436
  59.9 0.7 copy-start.7
  63.2 1.0 %copy-start.1 = (f32[3,512]{1,0:T(4,128)S(1)}, f32[3,512]{1,0:T(4,128)}, u32[]{:S(2)}) copy-start(f32[3,512]{1,0:T(4,128)} %param.17) | copy-start | bytes 18436
  63.5 16.1 %copy-start.3 = (f32[3,64]{1,0:T(4,128)S(1)}, f32[3,64]{1,0:T(4,128)}, u32[]{:S(2)}) copy-start(f32[3,64]{1,0:T(4,128)} %param.15) | copy-start | bytes 2308
  63.5 16.1 %copy-start.4 = (f32[3,64]{1,0:T(4,128)S(1)}, f32[3,64]{1,0:T(4,128)}, u32[]{:S(2)}) copy-start(f32[3,64]{1,0:T(4,128)} %param.14) | copy-start | bytes 2308
  63.6 16.1 %copy-start.5 = (f32[3,64]{1,0:T(4,128)S(1)}, f32[3,64]{1,0:T(4,128)}, u32[]{:S(2)}) copy-start(f32[3,64]{1,0:T(4,128)} %param.11) | copy-start | bytes 2308
  63.6 16.1 %copy-start.6 = (f32[3,64]{1,0:T(4,128)S(1)}, f32[3,64]{1,0:T(4,128)}, u32[]{:S(2)}) copy-start(f32[3,64]{1,0:T(4,128)} %param.12) | copy-start | bytes 2308
Sparse Core Ops, SparseCore 0:
  58.0 20.5 reduce-scatter.3
where the time goes:
time: 87.5 us; the launch traced here: 87.1 us
  blocking collectives  36.3 us (41%)
  between operations  14.3 us (16%)
  waiting for transfers between devices  13.6 us (16%)
  other arithmetic  8.23 us (9%)
  starting transfers between devices  7.32 us (8%)
  local copies, waits for them, and re-layouts  4.77 us (5%)
  matrix products  2.59 us (3%)
    all_gather x1, blocking collectives, body(): columns = lax.all_gather(own_state, 'wide', axis=1, tiled=True)  31.1 us
    unnamed x2, waiting for transfers between devices  13.6 us
    all_to_all x1, starting transfers between devices, body(): lax.all_to_all(outgoing, 'wide', split_axis=0, concat_axis=0, tiled=True)  7.28 us
    all_gather x1, blocking collectives, body(): sibling = lax.all_gather(own_state, 'narrow', axis=1, tiled=True)  5.19 us
    reduce_sum x4, other arithmetic, kernel(): return jnp.sum(offset * weight[None], axis=2)  1.95 us
    unnamed x23, local copies, waits for them, and re-layouts  1.92 us
  transfers between devices with their start and end apart: 2, of which 1 were waited for; matrix products, arithmetic and copies ran while one was open for 12% of the time, Pallas kernels for 0%

commit v1 on v0

v1 whole, which is shorter than its diff:
```python
import functools

import jax
import jax.numpy as jnp
from jax import lax
from jax.experimental import pallas as pl
from jax.experimental.pallas import tpu as pltpu
from jax.sharding import PartitionSpec as P

GROUPS = 32
LANES = 128
ROWS = 8
MESH = pl.DeviceIdType.MESH

time_step = 0.25
soften_sq = 0.05


def loop(count, step, init, most=4):
    unroll = next(u for u in range(min(most, count), 0, -1) if count % u == 0)
    return lax.fori_loop(0, count, step, init, unroll=unroll)


def spread(row):
    return jnp.broadcast_to(row, (ROWS, row.shape[1]))


def column(block, index):
    return jnp.broadcast_to(block[:, index : index + 1], (ROWS, LANES))


def pull(source, mass, target, total):
    dx, dy, dz = (s - t for s, t in zip(source, target))
    inverse = lax.rsqrt(dx * dx + dy * dy + dz * dz + soften_sq)
    weight = mass * inverse * inverse * inverse
    return (total[0] + dx * weight, total[1] + dy * weight, total[2] + dz * weight)


def kernel(
    n_wide,
    n_narrow,
    star_pos,
    star_vel,
    star_mass,
    star_acc,
    star_jerk,
    gal_pos,
    gal_vel,
    gal_mass,
    group_of,
    let_send,
    star_leaf,
    gal_out,
    pos_out,
    vel_out,
    own,
    states,
    cell_out,
    cell_in,
    cols,
    srow,
    crow,
    prow,
    send_sem,
    recv_sem,
    cell_send_sem,
    cell_recv_sem,
):
    n_dev = n_wide * n_narrow
    wide, narrow = lax.axis_index("wide"), lax.axis_index("narrow")
    me = wide * n_narrow + narrow
    stars = star_pos.shape[1]
    bodies = gal_pos.shape[1]
    leaves, kicks = star_leaf.shape
    slots = LANES // GROUPS
    step_sq = time_step * time_step

    barrier = pltpu.get_barrier_semaphore()

    def greet(i, carry):
        peer = lax.rem(me + i, n_dev)
        pl.semaphore_signal(
            barrier,
            inc=1,
            device_id=(peer // n_narrow, lax.rem(peer, n_narrow)),
            device_id_type=MESH,
        )
        return carry

    lax.fori_loop(1, n_dev, greet, 0)

    lane = lax.broadcasted_iota(jnp.int32, (1, LANES), 1)
    lane4 = lax.broadcasted_iota(jnp.int32, (4, LANES), 1)
    lane8 = lax.broadcasted_iota(jnp.int32, (ROWS, LANES), 1)
    row8 = lax.broadcasted_iota(jnp.int32, (ROWS, LANES), 0)
    left = lane4 < stars

    spos, svel = star_pos[...], star_vel[...]
    sacc, sjerk = star_acc[...], star_jerk[...]
    pred_pos = (
        spos + time_step * svel + step_sq * 0.5 * sacc + step_sq * time_step / 6.0 * sjerk
    )
    pred_vel = svel + time_step * sacc + step_sq * 0.5 * sjerk
    pos4 = jnp.concatenate([pred_pos, star_mass[...]], axis=0)
    vel4 = jnp.concatenate([pred_vel, jnp.zeros((1, stars), jnp.float32)], axis=0)
    block = jnp.concatenate([pos4, vel4], axis=1)
    parity = lax.rem(wide + narrow, 2)
    block = jnp.where(parity == 0, block, pltpu.roll(block, stars, 1))
    own[0] = block
    states[me] = block
    both = jnp.concatenate([pos4, vel4], axis=0)
    targets = jnp.transpose(
        jnp.concatenate([both, jnp.zeros((ROWS, LANES - stars), jnp.float32)], axis=1)
    )

    gpos, gmass = gal_pos[...], gal_mass[...]
    body_lane = lax.broadcasted_iota(jnp.int32, (1, bodies), 1)
    segment = group_of[...] + (body_lane // (bodies // leaves)) * GROUPS
    onehot = (
        lax.broadcasted_iota(jnp.int32, (LANES, bodies), 0)
        == jnp.broadcast_to(segment, (LANES, bodies))
    ).astype(jnp.float32)
    moments = jnp.concatenate(
        [gpos * gmass, gmass, jnp.zeros((4, bodies), jnp.float32)], axis=0
    )
    sums = lax.dot_general(
        moments,
        onehot,
        (((1,), (1,)), ((), ())),
        precision=lax.Precision.HIGHEST,
        preferred_element_type=jnp.float32,
    )
    cells = jnp.where(row8 < 3, sums / spread(sums[3:4]), sums)
    crow[0] = cells

    group = lane // GROUPS
    part = jnp.bitwise_and(group - lax.rem(wide, slots), slots - 1)
    chosen = let_send[...]
    outgoing = jnp.zeros((n_wide, LANES), jnp.float32)
    pick = jnp.bitwise_and(group - chosen, slots - 1)
    for k in range(slots):
        turned = cells if k == 0 else pltpu.roll(cells, k * GROUPS, 1)
        base = jnp.zeros((1, LANES), jnp.float32)
        for c in range(4):
            base = jnp.where(part == c, turned[c : c + 1], base)
        outgoing = jnp.where(
            jnp.logical_and(pick == k, chosen >= 0),
            jnp.broadcast_to(base, (n_wide, LANES)),
            outgoing,
        )
    cell_out[:, 0, :] = outgoing
    cell_in[wide] = jnp.zeros((1, LANES), jnp.float32)

    pl.semaphore_wait(barrier, n_dev - 1)

    def state_copy(peer):
        return pltpu.make_async_remote_copy(
            src_ref=own.at[0],
            dst_ref=states.at[me],
            send_sem=send_sem,
            recv_sem=recv_sem,
            device_id=(peer // n_narrow, lax.rem(peer, n_narrow)),
            device_id_type=MESH,
        )

    def cell_copy(other):
        return pltpu.make_async_remote_copy(
            src_ref=cell_out.at[other],
            dst_ref=cell_in.at[wide],
            send_sem=cell_send_sem,
            recv_sem=cell_recv_sem,
            device_id=(other, narrow),
            device_id_type=MESH,
        )

    def send_state(i, carry):
        state_copy(lax.rem(me + i, n_dev)).start()
        return carry

    def send_cell(i, carry):
        cell_copy(lax.rem(wide + i, n_wide)).start()
        return carry

    lax.fori_loop(1, n_wide, send_cell, 0)
    lax.fori_loop(1, n_dev, send_state, 0)

    tiles = bodies // LANES
    body_rows = jnp.concatenate(
        [gpos, gmass, jnp.zeros((4, bodies), jnp.float32)], axis=0
    )
    for t in range(tiles):
        cols[t * LANES : (t + 1) * LANES, :] = jnp.transpose(
            body_rows[:, t * LANES : (t + 1) * LANES]
        )
    here = [
        [spread(gpos[c : c + 1, t * LANES : (t + 1) * LANES]) for c in range(3)]
        for t in range(tiles)
    ]

    def on_bodies(start, which, total):
        source = cols[pl.ds(pl.multiple_of(start, ROWS), ROWS), :]
        place = [column(source, c) for c in range(3)]
        mass = column(source, 3)
        return tuple(pull(place, mass, here[t], total[i]) for i, t in enumerate(which))

    every = tuple(range(tiles))
    zero = jnp.zeros((ROWS, LANES), jnp.float32)
    total = tuple((zero, zero, zero) for _ in every)
    total = loop(bodies // ROWS, lambda g, acc: on_bodies(g * ROWS, every, acc), total)

    pltpu.make_async_copy(
        states.at[pl.ds(0, n_dev - 1)], states.at[pl.ds(0, n_dev - 1)], recv_sem
    ).wait()
    pltpu.make_async_copy(
        cell_in.at[pl.ds(0, n_wide - 1)], cell_in.at[pl.ds(0, n_wide - 1)], cell_recv_sem
    ).wait()

    odd = n_narrow // 2

    def star_rows(i, carry):
        w = i // odd
        first = w * n_narrow + 2 * lax.rem(i, odd)
        flip = lax.rem(w, 2)
        even_block, odd_block = states[first + flip], states[first + 1 - flip]
        srow[i, 0:4, :] = jnp.where(left, even_block, odd_block)
        srow[i, 4:8, :] = pltpu.roll(jnp.where(left, odd_block, even_block), stars, 1)
        return carry

    pairs = n_dev // 2
    loop(pairs, star_rows, 0, 16)

    flip = lax.rem(narrow, 2)

    def star_cols(i, carry):
        even_block = states[(2 * i + flip) * n_narrow + narrow]
        odd_block = states[(2 * i + 1 - flip) * n_narrow + narrow]
        rows = jnp.where(left, even_block, odd_block)
        rows = jnp.concatenate([rows, jnp.zeros((4, LANES), jnp.float32)], axis=0)
        start = pl.multiple_of(bodies + i * LANES, LANES)
        cols[pl.ds(start, LANES), :] = jnp.transpose(rows)
        return carry

    loop(n_wide // 2, star_cols, 0)

    ess_start = bodies + n_wide * stars

    def ess_rows(e, carry):
        parts = []
        for c in range(4):
            row = jnp.zeros((1, LANES), jnp.float32)
            for k in range(slots):
                row = jnp.where(group == (c + k) % slots, cell_in[e * slots + k], row)
            parts.append(row if c == 0 else pltpu.roll(row, LANES - c * GROUPS, 1))
        parts.append(jnp.zeros((4, LANES), jnp.float32))
        rows = jnp.concatenate(parts, axis=0)
        crow[e + 1] = rows
        start = pl.multiple_of(ess_start + e * LANES, LANES)
        cols[pl.ds(start, LANES), :] = jnp.transpose(rows)
        return carry

    loop(n_wide // slots, ess_rows, 0)

    pieces = []
    for t in range(0, stars, ROWS):
        mine = targets[t : t + ROWS, :]
        place = [column(mine, c) for c in range(3)]
        speed = [column(mine, 4 + c) for c in range(3)]

        def hermite(i, acc):
            rows = [spread(srow[i, c : c + 1, :]) for c in range(7)]
            dx, dy, dz = (rows[c] - place[c] for c in range(3))
            ux, uy, uz = (rows[4 + c] - speed[c] for c in range(3))
            inverse = lax.rsqrt(dx * dx + dy * dy + dz * dz + soften_sq)
            square = inverse * inverse
            weight = rows[3] * inverse * square
            approach = 3.0 * (dx * ux + dy * uy + dz * uz) * square
            return (
                acc[0] + dx * weight,
                acc[1] + dy * weight,
                acc[2] + dz * weight,
                acc[3] + (ux - dx * approach) * weight,
                acc[4] + (uy - dy * approach) * weight,
                acc[5] + (uz - dz * approach) * weight,
            )

        acc = loop(pairs, hermite, (zero,) * 6)

        def cell_pull(i, part):
            rows = [spread(crow[i, c : c + 1, :]) for c in range(4)]
            return pull(rows[:3], rows[3], place, part)

        acc = loop(n_wide // slots + 1, cell_pull, acc[:3]) + acc[3:]
        piece = jnp.zeros((ROWS, LANES), jnp.float32)
        for c in range(6):
            piece = jnp.where(lane8 == c, jnp.sum(acc[c], axis=1, keepdims=True), piece)
        pieces.append(piece)
    result = jnp.transpose(jnp.concatenate(pieces, axis=0))
    new_acc, new_jerk = result[0:3], result[3:6]
    vel_new = (
        svel + time_step * 0.5 * (sacc + new_acc) + step_sq / 12.0 * (sjerk - new_jerk)
    )
    vel_out[...] = vel_new
    pos_out[...] = (
        spos + time_step * 0.5 * (svel + vel_new) + step_sq / 12.0 * (sacc - new_acc)
    )

    if kicks == n_wide:
        total = loop(
            n_wide * stars // ROWS, lambda g, acc: on_bodies(bodies + g * ROWS, every, acc), total
        )
    else:
        kicked = []
        for t in every:

            def one_block(k, acc):
                listed = star_leaf[t * leaves // tiles, k]
                place = listed + flip - 2 * flip * lax.rem(listed, 2)
                start = bodies + place * stars
                return loop(
                    stars // ROWS, lambda g, part: on_bodies(start + g * ROWS, (t,), part), acc
                )

            kicked.append(lax.fori_loop(0, kicks, one_block, (total[t],))[0])
        total = tuple(kicked)
    total = loop(
        n_wide * GROUPS // ROWS, lambda g, acc: on_bodies(ess_start + g * ROWS, every, acc), total
    )
    for t in every:
        for c in range(3):
            piece = jnp.sum(total[t][c], axis=0, keepdims=True)
            spot = (slice(c, c + 1), slice(t * LANES, (t + 1) * LANES))
            gal_out[spot] = gal_vel[spot] + time_step * piece

    pltpu.make_async_copy(
        states.at[pl.ds(0, n_dev - 1)], states.at[pl.ds(0, n_dev - 1)], send_sem
    ).wait()
    pltpu.make_async_copy(
        cell_out.at[pl.ds(0, n_wide - 1)], cell_out.at[pl.ds(0, n_wide - 1)], cell_send_sem
    ).wait()


def body(
    n_wide,
    n_narrow,
    star_pos,
    star_vel,
    star_mass,
    star_acc,
    star_jerk,
    gal_pos,
    gal_vel,
    gal_mass,
    group_of,
    let_send,
    star_leaf,
):
    n_dev = n_wide * n_narrow
    stars, bodies = star_pos.shape[1], gal_pos.shape[1]
    vmem = pl.BlockSpec(memory_space=pltpu.VMEM)
    smem = pl.BlockSpec(memory_space=pltpu.SMEM)
    f32 = jnp.float32
    return pl.pallas_call(
        functools.partial(kernel, n_wide, n_narrow),
        out_shape=(
            jax.ShapeDtypeStruct(gal_vel.shape, f32),
            jax.ShapeDtypeStruct(star_pos.shape, f32),
            jax.ShapeDtypeStruct(star_vel.shape, f32),
        ),
        in_specs=[vmem] * 10 + [smem],
        out_specs=(vmem,) * 3,
        scratch_shapes=[
            pltpu.VMEM((1, 4, LANES), f32),
            pltpu.VMEM((n_dev, 4, LANES), f32),
            pltpu.VMEM((n_wide, 1, LANES), f32),
            pltpu.VMEM((n_wide, 1, LANES), f32),
            pltpu.VMEM((bodies + n_wide * (stars + GROUPS), ROWS), f32),
            pltpu.VMEM((n_dev // 2, ROWS, LANES), f32),
            pltpu.VMEM((n_wide * GROUPS // LANES + 1, ROWS, LANES), f32),
            pltpu.VMEM((ROWS, LANES), f32),
            pltpu.SemaphoreType.DMA,
            pltpu.SemaphoreType.DMA,
            pltpu.SemaphoreType.DMA,
            pltpu.SemaphoreType.DMA,
        ],
        compiler_params=pltpu.CompilerParams(collective_id=0, has_side_effects=True),
    )(
        star_pos,
        star_vel,
        star_mass.reshape(1, stars),
        star_acc,
        star_jerk,
        gal_pos,
        gal_vel,
        gal_mass.reshape(1, bodies),
        group_of.reshape(1, bodies),
        let_send.reshape(n_wide, 1),
        star_leaf,
    )


def solution(mesh):
    both = ("wide", "narrow")
    columns, flat = P(None, both), P(both)
    return jax.shard_map(
        functools.partial(body, mesh.shape["wide"], mesh.shape["narrow"]),
        mesh=mesh,
        in_specs=(
            columns,
            columns,
            flat,
            columns,
            columns,
            columns,
            columns,
            flat,
            flat,
            P(both, None, None),
            P(both, None),
        ),
        out_specs=(columns, columns, columns),
        check_vma=False,
    )
```

time: 87.5 us -> 21.1 us (0.24)
  blocking collectives: 36.3 us -> 0 us
  Pallas kernels: 0 us -> 16.3 us
  between operations: 14.3 us -> 0.66 us
  waiting for transfers between devices: 13.6 us -> 0 us
  other arithmetic: 8.23 us -> 0 us
  starting transfers between devices: 7.32 us -> 0 us
  matrix products: 2.59 us -> 0 us
  local copies, waits for them, and re-layouts: 4.77 us -> 3.88 us
    all_gather x2 -> x0, blocking collectives: 36.3 us -> none  [the longest x1 31.1 us: body(): columns = lax.all_gather(own_state, 'wide', axis=1, tiled=True)]
    pallas_call x0 -> x1, Pallas kernels: none -> 16.3 us  [body(): pl.pallas_call(functools.partial(kernel, n_wide, n_narrow), out_shape=(ja...]
    unnamed x2 -> x0, waiting for transfers between devices: 13.6 us -> none
    all_to_all x1 -> x0, starting transfers between devices: 7.28 us -> none  [body(): lax.all_to_all(outgoing, 'wide', split_axis=0, concat_axis=0, tiled=True)]
    reduce_sum x10 -> x0, other arithmetic: 4.18 us -> none  [the longest x4 1.95 us: kernel(): return jnp.sum(offset * weight[None], axis=2)]
    dot_general x3 -> x0, matrix products: 2.59 us -> none  [the longest x1 0.9 us: body(): jnp.einsum('lgb,clb->clg', onehot, leaf_pos * leaf_mass[None], precision=...]
    add x3 -> x0, other arithmetic: 1.94 us -> none  [the longest x1 0.74 us: body(): star_pos + time_step * star_vel + step_sq * 0.5 * star_acc]
    unnamed x23 -> x9, local copies, waits for them, and re-layouts: 1.92 us -> 3.21 us
  transfers between devices with their start and end apart: 2 -> 0, of which waited for: 1 -> 0; matrix products, arithmetic and copies ran while one was open for 12% -> 0% of each run, Pallas kernels for 0% -> 0%
where the time goes in v1:
time: 21.1 us; the launch traced here: 20.8 us
  Pallas kernels  16.3 us (77%)
  local copies, waits for them, and re-layouts  3.88 us (18%)
  between operations  0.66 us (3%)
    pallas_call x1, Pallas kernels, body(): pl.pallas_call(functools.partial(kernel, n_wide, n_narrow), out_shape=(ja...  16.3 us
    unnamed x9, local copies, waits for them, and re-layouts  3.21 us
    reshape x1, local copies, waits for them, and re-layouts, body(): let_send.reshape(n_wide, 1)  0.67 us

profile of v1, /device:TPU:0, one launch (start us, length us, event | category | flops | bytes accessed | tf_op | source)
XLA Modules:
  0.0 20.8 jit_solution(14676441821988525824)
XLA Ops:
  0.6 0.0 copy-start.2
  0.6 0.6 %copy-done.2 = s32[1,8,1]{1,2,0:T(1,128)S(1)} copy-done((s32[1,8,1]{1,2,0:T(1,128)S(1)}, s32[1,8,1]{1,2,0:T(1,128)}, u32[]{:S(2)}) %copy-start.2) | copy-done | bytes 56
  1.3 0.7 %copy.14.let_send = s32[8,1]{1,0:T(8,128)} copy(s32[8,1]{0,1:T(1,128)S(1)} %bitcast.7) | data formatting | bytes 64 | tf_op jit(solution)/shard_map/reshape | solution.py:396
  2.0 16.3 %shard_map.130 = (f32[3,512]{1,0:T(4,128)}, f32[3,64]{1,0:T(4,128)}, f32[3,64]{1,0:T(4,128)}) custom-call(f32[3,64]{1,0:T(4,128)} %star_pos.1, f32[3,64]{1,0:T(4,128)} %star_vel.1, f32[1,64]{1,0:T(1,128)} %bitcast.6, f32[3,64]{1,0:T(4,128)} %star_acc.1, f32[3,64]{1,0:T(4,128)} %star_jerk.1, f32[3,512]{1,0:T(4,128)} %gal_pos.1, f32[3,512]{1,0:T(4,128)} %gal_vel.1, ...), custom_call_target="tpu_custom_call" | custom-call | tf_op jit(solution)/shard_map/pallas_call | solution.py:362
  18.3 0.0 copy-start.1
  18.3 1.3 %copy.18 = f32[3,512]{1,0:T(4,128)} copy(f32[3,512]{1,0:T(4,128)} %get-tuple-element.6) | data formatting | bytes 12288
  19.6 0.0 copy-done.1
  19.6 0.0 copy-start
  19.6 0.6 %copy.19 = f32[3,64]{1,0:T(4,128)} copy(f32[3,64]{1,0:T(4,128)S(1)} %copy-done.1) | data formatting | bytes 1536
  20.2 0.1 copy-done
  20.3 0.6 %copy.20 = f32[3,64]{1,0:T(4,128)} copy(f32[3,64]{1,0:T(4,128)S(1)} %copy-done) | data formatting | bytes 1536
Async XLA Ops:
  0.6 0.7 %copy-start.2 = (s32[1,8,1]{1,2,0:T(1,128)S(1)}, s32[1,8,1]{1,2,0:T(1,128)}, u32[]{:S(2)}) copy-start(s32[1,8,1]{1,2,0:T(1,128)} %param.20) | copy-start | bytes 100
  18.3 1.3 %copy-start.1 = (f32[3,64]{1,0:T(4,128)S(1)}, f32[3,64]{1,0:T(4,128)}, u32[]{:S(2)}) copy-start(f32[3,64]{1,0:T(4,128)} %get-tuple-element.7) | copy-start | bytes 2308
  19.6 0.7 %copy-start = (f32[3,64]{1,0:T(4,128)S(1)}, f32[3,64]{1,0:T(4,128)}, u32[]{:S(2)}) copy-start(f32[3,64]{1,0:T(4,128)} %get-tuple-element.8) | copy-start | bytes 2308

commit v2 on v1

--- a/solution.py
+++ b/solution.py
@@ -39,6 +39,18 @@
 def kernel(
     n_wide,
     n_narrow,
+    star_pos_hbm,
+    star_vel_hbm,
+    star_mass_hbm,
+    star_acc_hbm,
+    star_jerk_hbm,
+    gal_pos_hbm,
+    gal_vel_hbm,
+    gal_mass_hbm,
+    group_of_hbm,
+    let_send_hbm,
+    star_leaf_hbm,
+    out,
     star_pos,
     star_vel,
     star_mass,
@@ -50,9 +62,7 @@
     group_of,
     let_send,
     star_leaf,
-    gal_out,
-    pos_out,
-    vel_out,
+    in_sem,
     own,
     states,
     cell_out,
@@ -60,7 +70,6 @@
     cols,
     srow,
     crow,
-    prow,
     send_sem,
     recv_sem,
     cell_send_sem,
@@ -75,6 +84,27 @@
     slots = LANES // GROUPS
     step_sq = time_step * time_step
 
+    fetches = [
+        pltpu.make_async_copy(source, target, in_sem.at[i])
+        for i, (source, target) in enumerate(
+            (
+                (star_pos_hbm, star_pos),
+                (star_vel_hbm, star_vel),
+                (star_mass_hbm, star_mass),
+                (star_acc_hbm, star_acc),
+                (star_jerk_hbm, star_jerk),
+                (gal_pos_hbm, gal_pos),
+                (gal_vel_hbm, gal_vel),
+                (gal_mass_hbm, gal_mass),
+                (group_of_hbm, group_of),
+                (let_send_hbm, let_send),
+                (star_leaf_hbm, star_leaf),
+            )
+        )
+    ]
+    for fetch in fetches:
+        fetch.start()
+
     barrier = pltpu.get_barrier_semaphore()
 
     def greet(i, carry):
@@ -94,6 +124,9 @@
     lane8 = lax.broadcasted_iota(jnp.int32, (ROWS, LANES), 1)
     row8 = lax.broadcasted_iota(jnp.int32, (ROWS, LANES), 0)
     left = lane4 < stars
+
+    for fetch in fetches:
+        fetch.wait()
 
     spos, svel = star_pos[...], star_vel[...]
     sacc, sjerk = star_acc[...], star_jerk[...]
@@ -135,7 +168,13 @@
 
     group = lane // GROUPS
     part = jnp.bitwise_and(group - lax.rem(wide, slots), slots - 1)
-    chosen = let_send[...]
+    square = (n_wide, n_wide)
+    diagonal = lax.broadcasted_iota(jnp.int32, square, 0) == lax.broadcasted_iota(
+        jnp.int32, square, 1
+    )
+    listed = jnp.broadcast_to(let_send[...].astype(jnp.float32), square)
+    chosen = jnp.sum(jnp.where(diagonal, listed, 0.0), axis=1, keepdims=True)
+    chosen = jnp.broadcast_to(chosen, (n_wide, LANES)).astype(jnp.int32)
     outgoing = jnp.zeros((n_wide, LANES), jnp.float32)
     pick = jnp.bitwise_and(group - chosen, slots - 1)
     for k in range(slots):
@@ -299,8 +338,9 @@
     vel_new = (
         svel + time_step * 0.5 * (sacc + new_acc) + step_sq / 12.0 * (sjerk - new_jerk)
     )
-    vel_out[...] = vel_new
-    pos_out[...] = (
+    vel_at = bodies + LANES
+    out[:, vel_at : vel_at + stars] = vel_new
+    out[:, bodies : bodies + stars] = (
         spos + time_step * 0.5 * (svel + vel_new) + step_sq / 12.0 * (sacc - new_acc)
     )
 
@@ -329,7 +369,7 @@
         for c in range(3):
             piece = jnp.sum(total[t][c], axis=0, keepdims=True)
             spot = (slice(c, c + 1), slice(t * LANES, (t + 1) * LANES))
-            gal_out[spot] = gal_vel[spot] + time_step * piece
+            out[spot] = gal_vel[spot] + time_step * piece
 
     pltpu.make_async_copy(
         states.at[pl.ds(0, n_dev - 1)], states.at[pl.ds(0, n_dev - 1)], send_sem
@@ -337,6 +377,13 @@
     pltpu.make_async_copy(
         cell_out.at[pl.ds(0, n_wide - 1)], cell_out.at[pl.ds(0, n_wide - 1)], cell_send_sem
     ).wait()
+
+
+def unpack(packed, gal_out, pos_out, vel_out):
+    bodies, stars = gal_out.shape[1], pos_out.shape[1]
+    gal_out[...] = packed[:, 0:bodies]
+    pos_out[...] = packed[:, bodies : bodies + stars]
+    vel_out[...] = packed[:, bodies + LANES : bodies + LANES + stars]
 
 
 def body(
@@ -357,18 +404,27 @@
     n_dev = n_wide * n_narrow
     stars, bodies = star_pos.shape[1], gal_pos.shape[1]
     vmem = pl.BlockSpec(memory_space=pltpu.VMEM)
-    smem = pl.BlockSpec(memory_space=pltpu.SMEM)
     f32 = jnp.float32
-    return pl.pallas_call(
+    i32 = jnp.int32
+    hbm = pl.BlockSpec(memory_space=pltpu.HBM)
+    packed = pl.pallas_call(
         functools.partial(kernel, n_wide, n_narrow),
-        out_shape=(
-            jax.ShapeDtypeStruct(gal_vel.shape, f32),
-            jax.ShapeDtypeStruct(star_pos.shape, f32),
-            jax.ShapeDtypeStruct(star_vel.shape, f32),
-        ),
-        in_specs=[vmem] * 10 + [smem],
-        out_specs=(vmem,) * 3,
+        out_shape=jax.ShapeDtypeStruct((3, bodies + 2 * LANES), f32),
+        in_specs=[hbm] * 11,
+        out_specs=vmem,
         scratch_shapes=[
+            pltpu.VMEM((3, stars), f32),
+            pltpu.VMEM((3, stars), f32),
+            pltpu.VMEM((1, stars), f32),
+            pltpu.VMEM((3, stars), f32),
+            pltpu.VMEM((3, stars), f32),
+            pltpu.VMEM((3, bodies), f32),
+            pltpu.VMEM((3, bodies), f32),
+            pltpu.VMEM((1, bodies), f32),
+            pltpu.VMEM((1, bodies), i32),
+            pltpu.VMEM((1, n_wide), i32),
+            pltpu.SMEM(star_leaf.shape, i32),
+            pltpu.SemaphoreType.DMA((11,)),
             pltpu.VMEM((1, 4, LANES), f32),
             pltpu.VMEM((n_dev, 4, LANES), f32),
             pltpu.VMEM((n_wide, 1, LANES), f32),
@@ -376,26 +432,43 @@
             pltpu.VMEM((bodies + n_wide * (stars + GROUPS), ROWS), f32),
             pltpu.VMEM((n_dev // 2, ROWS, LANES), f32),
             pltpu.VMEM((n_wide * GROUPS // LANES + 1, ROWS, LANES), f32),
-            pltpu.VMEM((ROWS, LANES), f32),
             pltpu.SemaphoreType.DMA,
             pltpu.SemaphoreType.DMA,
             pltpu.SemaphoreType.DMA,
             pltpu.SemaphoreType.DMA,
         ],
-        compiler_params=pltpu.CompilerParams(collective_id=0, has_side_effects=True),
+        compiler_params=pltpu.CompilerParams(
+            collective_id=0, has_side_effects=True, vmem_limit_bytes=24 << 20
+        ),
     )(
-        star_pos,
-        star_vel,
-        star_mass.reshape(1, stars),
-        star_acc,
-        star_jerk,
-        gal_pos,
-        gal_vel,
-        gal_mass.reshape(1, bodies),
-        group_of.reshape(1, bodies),
-        let_send.reshape(n_wide, 1),
-        star_leaf,
-    )
+        *(
+            pltpu.with_memory_space_constraint(array, pltpu.HBM)
+            for array in (
+                star_pos,
+                star_vel,
+                star_mass.reshape(1, stars),
+                star_acc,
+                star_jerk,
+                gal_pos,
+                gal_vel,
+                gal_mass.reshape(1, bodies),
+                group_of.reshape(1, bodies),
+                let_send.reshape(1, n_wide),
+                star_leaf,
+            )
+        )
+    )
+    return pl.pallas_call(
+        unpack,
+        out_shape=(
+            jax.ShapeDtypeStruct(gal_vel.shape, f32),
+            jax.ShapeDtypeStruct(star_pos.shape, f32),
+            jax.ShapeDtypeStruct(star_vel.shape, f32),
+        ),
+        in_specs=[vmem],
+        out_specs=(vmem,) * 3,
+        compiler_params=pltpu.CompilerParams(vmem_limit_bytes=1 << 20),
+    )(packed)
 
 
 def solution(mesh):

time: 21.1 us -> 16.5 us (0.78)
  local copies, waits for them, and re-layouts: 3.88 us -> 0 us
  Pallas kernels: 16.3 us -> 15.7 us
    unnamed x9 -> x0, local copies, waits for them, and re-layouts: 3.21 us -> none
    reshape x1 -> x0, local copies, waits for them, and re-layouts: 0.67 us -> none  [body(): let_send.reshape(n_wide, 1)]
    pallas_call x1 -> x2, Pallas kernels: 16.3 us -> 15.7 us  [the longest x1 15.1 us: body(): pl.pallas_call(functools.partial(kernel, n_wide, n_narrow), out_shape=jax...]
where the time goes in v2:
time: 16.5 us; the launch traced here: 16.4 us
  Pallas kernels  15.7 us (95%)
  between operations  0.64 us (4%)
    pallas_call x1, Pallas kernels, body(): pl.pallas_call(functools.partial(kernel, n_wide, n_narrow), out_shape=jax...  15.1 us
    pallas_call x1, Pallas kernels, body(): pl.pallas_call(unpack, out_shape=(jax.ShapeDtypeStruct(gal_vel.shape, f32...  0.61 us

profile of v2, /device:TPU:0, one launch (start us, length us, event | category | flops | bytes accessed | tf_op | source)
XLA Modules:
  0.0 16.4 jit_solution(13826671065350911044)
XLA Ops:
  0.6 15.1 %shard_map.130.packed = f32[3,768]{1,0:T(4,128)S(1)} custom-call(f32[3,64]{1,0:T(4,128)} %star_pos_hbm.1, f32[3,64]{1,0:T(4,128)} %star_vel_hbm.1, f32[1,64]{1,0:T(1,128)} %bitcast.6, f32[3,64]{1,0:T(4,128)} %star_acc_hbm.1, f32[3,64]{1,0:T(4,128)} %star_jerk_hbm.1, f32[3,512]{1,0:T(4,128)} %gal_pos_hbm.1, f32[3,512]{1,0:T(4,128)} %gal_vel_hbm.1, ...), custom_call_target="tpu_custom_call" | custom-call | tf_op jit(solution)/shard_map/pallas_call | solution.py:410
  15.7 0.6 %shard_map.131 = (f32[3,512]{1,0:T(4,128)}, f32[3,64]{1,0:T(4,128)}, f32[3,64]{1,0:T(4,128)}) custom-call(f32[3,768]{1,0:T(4,128)S(1)} %shard_map.130.packed), custom_call_target="tpu_custom_call" | custom-call | tf_op jit(solution)/shard_map/pallas_call | solution.py:461

commit v3 on v2

--- a/solution.py
+++ b/solution.py
@@ -63,7 +63,6 @@
     let_send,
     star_leaf,
     in_sem,
-    own,
     states,
     cell_out,
     cell_in,
@@ -74,10 +73,10 @@
     recv_sem,
     cell_send_sem,
     cell_recv_sem,
+    pass_send_sem,
+    pass_recv_sem,
 ):
-    n_dev = n_wide * n_narrow
     wide, narrow = lax.axis_index("wide"), lax.axis_index("narrow")
-    me = wide * n_narrow + narrow
     stars = star_pos.shape[1]
     bodies = gal_pos.shape[1]
     leaves, kicks = star_leaf.shape
@@ -107,17 +106,16 @@
 
     barrier = pltpu.get_barrier_semaphore()
 
-    def greet(i, carry):
-        peer = lax.rem(me + i, n_dev)
-        pl.semaphore_signal(
-            barrier,
-            inc=1,
-            device_id=(peer // n_narrow, lax.rem(peer, n_narrow)),
-            device_id_type=MESH,
-        )
+    def greet(w, n):
+        pl.semaphore_signal(barrier, inc=1, device_id=(w, n), device_id_type=MESH)
+
+    def greet_wide(i, carry):
+        greet(lax.rem(wide + i, n_wide), narrow)
         return carry
 
-    lax.fori_loop(1, n_dev, greet, 0)
+    lax.fori_loop(1, n_wide, greet_wide, 0)
+    for i in range(1, n_narrow):
+        greet(wide, lax.rem(narrow + i, n_narrow))
 
     lane = lax.broadcasted_iota(jnp.int32, (1, LANES), 1)
     lane4 = lax.broadcasted_iota(jnp.int32, (4, LANES), 1)
@@ -137,10 +135,8 @@
     pos4 = jnp.concatenate([pred_pos, star_mass[...]], axis=0)
     vel4 = jnp.concatenate([pred_vel, jnp.zeros((1, stars), jnp.float32)], axis=0)
     block = jnp.concatenate([pos4, vel4], axis=1)
-    parity = lax.rem(wide + narrow, 2)
-    block = jnp.where(parity == 0, block, pltpu.roll(block, stars, 1))
-    own[0] = block
-    states[me] = block
+    block = jnp.where(lax.rem(wide, 2) == 0, block, pltpu.roll(block, stars, 1))
+    states[narrow, wide] = block
     both = jnp.concatenate([pos4, vel4], axis=0)
     targets = jnp.transpose(
         jnp.concatenate([both, jnp.zeros((ROWS, LANES - stars), jnp.float32)], axis=1)
@@ -190,38 +186,29 @@
     cell_out[:, 0, :] = outgoing
     cell_in[wide] = jnp.zeros((1, LANES), jnp.float32)
 
-    pl.semaphore_wait(barrier, n_dev - 1)
-
-    def state_copy(peer):
-        return pltpu.make_async_remote_copy(
-            src_ref=own.at[0],
-            dst_ref=states.at[me],
+    pl.semaphore_wait(barrier, n_wide + n_narrow - 2)
+
+    def send_wide(i, carry):
+        peer = (lax.rem(wide + i, n_wide), narrow)
+        pltpu.make_async_remote_copy(
+            src_ref=states.at[narrow, wide],
+            dst_ref=states.at[narrow, wide],
             send_sem=send_sem,
             recv_sem=recv_sem,
-            device_id=(peer // n_narrow, lax.rem(peer, n_narrow)),
+            device_id=peer,
             device_id_type=MESH,
-        )
-
-    def cell_copy(other):
-        return pltpu.make_async_remote_copy(
-            src_ref=cell_out.at[other],
+        ).start()
+        pltpu.make_async_remote_copy(
+            src_ref=cell_out.at[peer[0]],
             dst_ref=cell_in.at[wide],
             send_sem=cell_send_sem,
             recv_sem=cell_recv_sem,
-            device_id=(other, narrow),
+            device_id=peer,
             device_id_type=MESH,
-        )
-
-    def send_state(i, carry):
-        state_copy(lax.rem(me + i, n_dev)).start()
+        ).start()
         return carry
 
-    def send_cell(i, carry):
-        cell_copy(lax.rem(wide + i, n_wide)).start()
-        return carry
-
-    lax.fori_loop(1, n_wide, send_cell, 0)
-    lax.fori_loop(1, n_dev, send_state, 0)
+    lax.fori_loop(1, n_wide, send_wide, 0)
 
     tiles = bodies // LANES
     body_rows = jnp.concatenate(
@@ -247,39 +234,39 @@
     total = tuple((zero, zero, zero) for _ in every)
     total = loop(bodies // ROWS, lambda g, acc: on_bodies(g * ROWS, every, acc), total)
 
-    pltpu.make_async_copy(
-        states.at[pl.ds(0, n_dev - 1)], states.at[pl.ds(0, n_dev - 1)], recv_sem
-    ).wait()
-    pltpu.make_async_copy(
-        cell_in.at[pl.ds(0, n_wide - 1)], cell_in.at[pl.ds(0, n_wide - 1)], cell_recv_sem
-    ).wait()
-
-    odd = n_narrow // 2
-
-    def star_rows(i, carry):
-        w = i // odd
-        first = w * n_narrow + 2 * lax.rem(i, odd)
-        flip = lax.rem(w, 2)
-        even_block, odd_block = states[first + flip], states[first + 1 - flip]
-        srow[i, 0:4, :] = jnp.where(left, even_block, odd_block)
-        srow[i, 4:8, :] = pltpu.roll(jnp.where(left, odd_block, even_block), stars, 1)
-        return carry
-
-    pairs = n_dev // 2
-    loop(pairs, star_rows, 0, 16)
-
-    flip = lax.rem(narrow, 2)
+    some = states.at[0, pl.ds(0, n_wide - 1)]
+    pltpu.make_async_copy(some, some, recv_sem).wait()
+    for i in range(1, n_narrow):
+        pltpu.make_async_remote_copy(
+            src_ref=states.at[narrow],
+            dst_ref=states.at[narrow],
+            send_sem=pass_send_sem,
+            recv_sem=pass_recv_sem,
+            device_id=(wide, lax.rem(narrow + i, n_narrow)),
+            device_id_type=MESH,
+        ).start()
+
+    halves = n_wide // 2
+
+    def star_rows(n, i):
+        even_block, odd_block = states[n, 2 * i], states[n, 2 * i + 1]
+        rows = jnp.where(left, even_block, odd_block)
+        spot = n * halves + i
+        srow[spot, 0:4, :] = rows
+        srow[spot, 4:8, :] = pltpu.roll(jnp.where(left, odd_block, even_block), stars, 1)
+        return rows
 
     def star_cols(i, carry):
-        even_block = states[(2 * i + flip) * n_narrow + narrow]
-        odd_block = states[(2 * i + 1 - flip) * n_narrow + narrow]
-        rows = jnp.where(left, even_block, odd_block)
-        rows = jnp.concatenate([rows, jnp.zeros((4, LANES), jnp.float32)], axis=0)
+        rows = jnp.concatenate(
+            [star_rows(narrow, i), jnp.zeros((4, LANES), jnp.float32)], axis=0
+        )
         start = pl.multiple_of(bodies + i * LANES, LANES)
         cols[pl.ds(start, LANES), :] = jnp.transpose(rows)
         return carry
 
-    loop(n_wide // 2, star_cols, 0)
+    loop(halves, star_cols, 0)
+    few = cell_in.at[pl.ds(0, n_wide - 1)]
+    pltpu.make_async_copy(few, few, cell_recv_sem).wait()
 
     ess_start = bodies + n_wide * stars
 
@@ -298,6 +285,43 @@
         return carry
 
     loop(n_wide // slots, ess_rows, 0)
+
+    if kicks == n_wide:
+        total = loop(
+            n_wide * stars // ROWS, lambda g, acc: on_bodies(bodies + g * ROWS, every, acc), total
+        )
+    else:
+        kicked = []
+        for t in every:
+
+            def one_block(k, acc):
+                listed = star_leaf[t * leaves // tiles, k]
+                start = bodies + listed * stars
+                return loop(
+                    stars // ROWS, lambda g, part: on_bodies(start + g * ROWS, (t,), part), acc
+                )
+
+            kicked.append(lax.fori_loop(0, kicks, one_block, (total[t],))[0])
+        total = tuple(kicked)
+    total = loop(
+        n_wide * GROUPS // ROWS, lambda g, acc: on_bodies(ess_start + g * ROWS, every, acc), total
+    )
+    for t in every:
+        for c in range(3):
+            piece = jnp.sum(total[t][c], axis=0, keepdims=True)
+            spot = (slice(c, c + 1), slice(t * LANES, (t + 1) * LANES))
+            out[spot] = gal_vel[spot] + time_step * piece
+
+    rest = states.at[pl.ds(0, n_narrow - 1)]
+    pltpu.make_async_copy(rest, rest, pass_recv_sem).wait()
+
+    def passed_rows(i, carry):
+        n = lax.rem(narrow + 1 + i // halves, n_narrow)
+        star_rows(n, lax.rem(i, halves))
+        return carry
+
+    loop((n_narrow - 1) * halves, passed_rows, 0, 12)
+    pairs = n_narrow * halves
 
     pieces = []
     for t in range(0, stars, ROWS):
@@ -344,39 +368,9 @@
         spos + time_step * 0.5 * (svel + vel_new) + step_sq / 12.0 * (sacc - new_acc)
     )
 
-    if kicks == n_wide:
-        total = loop(
-            n_wide * stars // ROWS, lambda g, acc: on_bodies(bodies + g * ROWS, every, acc), total
-        )
-    else:
-        kicked = []
-        for t in every:
-
-            def one_block(k, acc):
-                listed = star_leaf[t * leaves // tiles, k]
-                place = listed + flip - 2 * flip * lax.rem(listed, 2)
-                start = bodies + place * stars
-                return loop(
-                    stars // ROWS, lambda g, part: on_bodies(start + g * ROWS, (t,), part), acc
-                )
-
-            kicked.append(lax.fori_loop(0, kicks, one_block, (total[t],))[0])
-        total = tuple(kicked)
-    total = loop(
-        n_wide * GROUPS // ROWS, lambda g, acc: on_bodies(ess_start + g * ROWS, every, acc), total
-    )
-    for t in every:
-        for c in range(3):
-            piece = jnp.sum(total[t][c], axis=0, keepdims=True)
-            spot = (slice(c, c + 1), slice(t * LANES, (t + 1) * LANES))
-            out[spot] = gal_vel[spot] + time_step * piece
-
-    pltpu.make_async_copy(
-        states.at[pl.ds(0, n_dev - 1)], states.at[pl.ds(0, n_dev - 1)], send_sem
-    ).wait()
-    pltpu.make_async_copy(
-        cell_out.at[pl.ds(0, n_wide - 1)], cell_out.at[pl.ds(0, n_wide - 1)], cell_send_sem
-    ).wait()
+    pltpu.make_async_copy(some, some, send_sem).wait()
+    pltpu.make_async_copy(few, few, cell_send_sem).wait()
+    pltpu.make_async_copy(rest, rest, pass_send_sem).wait()
 
 
 def unpack(packed, gal_out, pos_out, vel_out):
@@ -425,13 +419,14 @@
             pltpu.VMEM((1, n_wide), i32),
             pltpu.SMEM(star_leaf.shape, i32),
             pltpu.SemaphoreType.DMA((11,)),
-            pltpu.VMEM((1, 4, LANES), f32),
-            pltpu.VMEM((n_dev, 4, LANES), f32),
+            pltpu.VMEM((n_narrow, n_wide, 4, LANES), f32),
             pltpu.VMEM((n_wide, 1, LANES), f32),
             pltpu.VMEM((n_wide, 1, LANES), f32),
             pltpu.VMEM((bodies + n_wide * (stars + GROUPS), ROWS), f32),
             pltpu.VMEM((n_dev // 2, ROWS, LANES), f32),
             pltpu.VMEM((n_wide * GROUPS // LANES + 1, ROWS, LANES), f32),
+            pltpu.SemaphoreType.DMA,
+            pltpu.SemaphoreType.DMA,
             pltpu.SemaphoreType.DMA,
             pltpu.SemaphoreType.DMA,
             pltpu.SemaphoreType.DMA,

time: 16.5 us -> 16 us (0.970)
  Pallas kernels: 15.7 us -> 15.2 us
    pallas_call x1, Pallas kernels: 15.1 us -> 14.6 us  [body(): pl.pallas_call(functools.partial(kernel, n_wide, n_narrow), out_shape=jax...]
where the time goes in v3:
time: 16 us; the launch traced here: 15.8 us
  Pallas kernels  15.2 us (95%)
  between operations  0.64 us (4%)
    pallas_call x1, Pallas kernels, body(): pl.pallas_call(functools.partial(kernel, n_wide, n_narrow), out_shape=jax...  14.6 us
    pallas_call x1, Pallas kernels, body(): pl.pallas_call(unpack, out_shape=(jax.ShapeDtypeStruct(gal_vel.shape, f32...  0.61 us

profile of v3, /device:TPU:0, one launch (start us, length us, event | category | flops | bytes accessed | tf_op | source)
XLA Modules:
  0.0 15.8 jit_solution(3117629735250671780)
XLA Ops:
  0.6 14.6 %shard_map.130.packed = f32[3,768]{1,0:T(4,128)S(1)} custom-call(f32[3,64]{1,0:T(4,128)} %star_pos_hbm.1, f32[3,64]{1,0:T(4,128)} %star_vel_hbm.1, f32[1,64]{1,0:T(1,128)} %bitcast.6, f32[3,64]{1,0:T(4,128)} %star_acc_hbm.1, f32[3,64]{1,0:T(4,128)} %star_jerk_hbm.1, f32[3,512]{1,0:T(4,128)} %gal_pos_hbm.1, f32[3,512]{1,0:T(4,128)} %gal_vel_hbm.1, ...), custom_call_target="tpu_custom_call" | custom-call | tf_op jit(solution)/shard_map/pallas_call | solution.py:404
  15.2 0.6 %shard_map.131 = (f32[3,512]{1,0:T(4,128)}, f32[3,64]{1,0:T(4,128)}, f32[3,64]{1,0:T(4,128)}) custom-call(f32[3,768]{1,0:T(4,128)S(1)} %shard_map.130.packed), custom_call_target="tpu_custom_call" | custom-call | tf_op jit(solution)/shard_map/pallas_call | solution.py:456

commit v4 on v3

--- a/solution.py
+++ b/solution.py
@@ -10,6 +10,8 @@
 GROUPS = 32
 LANES = 128
 ROWS = 8
+BODY_UNROLL = 16
+STAR_UNROLL = 16
 MESH = pl.DeviceIdType.MESH
 
 time_step = 0.25
@@ -109,13 +111,20 @@
     def greet(w, n):
         pl.semaphore_signal(barrier, inc=1, device_id=(w, n), device_id_type=MESH)
 
-    def greet_wide(i, carry):
-        greet(lax.rem(wide + i, n_wide), narrow)
+    beside = [narrow] + [lax.rem(narrow + m, n_narrow) for m in range(1, n_narrow)]
+
+    def each_wide(first, step):
+        lax.fori_loop(first, n_wide, step, 0, unroll=n_wide <= 16)
+
+    def greet_peers(j, carry):
+        w = lax.rem(wide + j, n_wide)
+        for n in beside:
+            greet(w, n)
         return carry
 
-    lax.fori_loop(1, n_wide, greet_wide, 0)
-    for i in range(1, n_narrow):
-        greet(wide, lax.rem(narrow + i, n_narrow))
+    each_wide(1, greet_peers)
+    for n in beside[1:]:
+        greet(wide, n)
 
     lane = lax.broadcasted_iota(jnp.int32, (1, LANES), 1)
     lane4 = lax.broadcasted_iota(jnp.int32, (4, LANES), 1)
@@ -186,29 +195,41 @@
     cell_out[:, 0, :] = outgoing
     cell_in[wide] = jnp.zeros((1, LANES), jnp.float32)
 
-    pl.semaphore_wait(barrier, n_wide + n_narrow - 2)
-
-    def send_wide(i, carry):
-        peer = (lax.rem(wide + i, n_wide), narrow)
+    pl.semaphore_wait(barrier, n_wide * n_narrow - 1)
+
+    def send_state(w, n, sends, recvs):
         pltpu.make_async_remote_copy(
             src_ref=states.at[narrow, wide],
             dst_ref=states.at[narrow, wide],
-            send_sem=send_sem,
-            recv_sem=recv_sem,
-            device_id=peer,
+            send_sem=sends,
+            recv_sem=recvs,
+            device_id=(w, n),
             device_id_type=MESH,
         ).start()
+
+    def send_wide(j, carry):
+        w = lax.rem(wide + j, n_wide)
         pltpu.make_async_remote_copy(
-            src_ref=cell_out.at[peer[0]],
+            src_ref=cell_out.at[w],
             dst_ref=cell_in.at[wide],
             send_sem=cell_send_sem,
             recv_sem=cell_recv_sem,
-            device_id=peer,
+            device_id=(w, narrow),
             device_id_type=MESH,
         ).start()
+        send_state(w, narrow, send_sem, recv_sem)
         return carry
 
-    lax.fori_loop(1, n_wide, send_wide, 0)
+    def send_others(j, carry):
+        w = lax.rem(wide + j, n_wide)
+        for n in beside[1:]:
+            send_state(w, n, pass_send_sem, pass_recv_sem)
+        return carry
+
+    each_wide(1, send_wide)
+    each_wide(1, send_others)
+    for n in beside[1:]:
+        send_state(wide, n, pass_send_sem, pass_recv_sem)
 
     tiles = bodies // LANES
     body_rows = jnp.concatenate(
@@ -232,20 +253,10 @@
     every = tuple(range(tiles))
     zero = jnp.zeros((ROWS, LANES), jnp.float32)
     total = tuple((zero, zero, zero) for _ in every)
-    total = loop(bodies // ROWS, lambda g, acc: on_bodies(g * ROWS, every, acc), total)
+    total = loop(bodies // ROWS, lambda g, acc: on_bodies(g * ROWS, every, acc), total, BODY_UNROLL)
 
     some = states.at[0, pl.ds(0, n_wide - 1)]
     pltpu.make_async_copy(some, some, recv_sem).wait()
-    for i in range(1, n_narrow):
-        pltpu.make_async_remote_copy(
-            src_ref=states.at[narrow],
-            dst_ref=states.at[narrow],
-            send_sem=pass_send_sem,
-            recv_sem=pass_recv_sem,
-            device_id=(wide, lax.rem(narrow + i, n_narrow)),
-            device_id_type=MESH,
-        ).start()
-
     halves = n_wide // 2
 
     def star_rows(n, i):
@@ -287,10 +298,9 @@
     loop(n_wide // slots, ess_rows, 0)
 
     if kicks == n_wide:
-        total = loop(
-            n_wide * stars // ROWS, lambda g, acc: on_bodies(bodies + g * ROWS, every, acc), total
-        )
+        shared = bodies
     else:
+        shared = ess_start
         kicked = []
         for t in every:
 
@@ -304,7 +314,10 @@
             kicked.append(lax.fori_loop(0, kicks, one_block, (total[t],))[0])
         total = tuple(kicked)
     total = loop(
-        n_wide * GROUPS // ROWS, lambda g, acc: on_bodies(ess_start + g * ROWS, every, acc), total
+        (ess_start + n_wide * GROUPS - shared) // ROWS,
+        lambda g, acc: on_bodies(shared + g * ROWS, every, acc),
+        total,
+        BODY_UNROLL,
     )
     for t in every:
         for c in range(3):
@@ -346,7 +359,7 @@
                 acc[5] + (uz - dz * approach) * weight,
             )
 
-        acc = loop(pairs, hermite, (zero,) * 6)
+        acc = loop(pairs, hermite, (zero,) * 6, STAR_UNROLL)
 
         def cell_pull(i, part):
             rows = [spread(crow[i, c : c + 1, :]) for c in range(4)]

time: 16 us -> 14 us (0.88)
  Pallas kernels: 15.2 us -> 13.2 us
    pallas_call x1, Pallas kernels: 14.6 us -> 12.6 us  [body(): pl.pallas_call(functools.partial(kernel, n_wide, n_narrow), out_shape=jax...]
where the time goes in v4:
time: 14 us; the launch traced here: 13.8 us
  Pallas kernels  13.2 us (94%)
  between operations  0.64 us (5%)
    pallas_call x1, Pallas kernels, body(): pl.pallas_call(functools.partial(kernel, n_wide, n_narrow), out_shape=jax...  12.6 us
    pallas_call x1, Pallas kernels, body(): pl.pallas_call(unpack, out_shape=(jax.ShapeDtypeStruct(gal_vel.shape, f32...  0.61 us

profile of v4, /device:TPU:0, one launch (start us, length us, event | category | flops | bytes accessed | tf_op | source)
XLA Modules:
  0.0 13.8 jit_solution(11922857652064041553)
XLA Ops:
  0.6 12.6 %shard_map.130.packed = f32[3,768]{1,0:T(4,128)S(1)} custom-call(f32[3,64]{1,0:T(4,128)} %star_pos_hbm.1, f32[3,64]{1,0:T(4,128)} %star_vel_hbm.1, f32[1,64]{1,0:T(1,128)} %bitcast.6, f32[3,64]{1,0:T(4,128)} %star_acc_hbm.1, f32[3,64]{1,0:T(4,128)} %star_jerk_hbm.1, f32[3,512]{1,0:T(4,128)} %gal_pos_hbm.1, f32[3,512]{1,0:T(4,128)} %gal_vel_hbm.1, ...), custom_call_target="tpu_custom_call" | custom-call | tf_op jit(solution)/shard_map/pallas_call | solution.py:417
  13.2 0.6 %shard_map.131 = (f32[3,512]{1,0:T(4,128)}, f32[3,64]{1,0:T(4,128)}, f32[3,64]{1,0:T(4,128)}) custom-call(f32[3,768]{1,0:T(4,128)S(1)} %shard_map.130.packed), custom_call_target="tpu_custom_call" | custom-call | tf_op jit(solution)/shard_map/pallas_call | solution.py:469

commit v5 on v4

--- a/solution.py
+++ b/solution.py
@@ -10,7 +10,7 @@
 GROUPS = 32
 LANES = 128
 ROWS = 8
-BODY_UNROLL = 16
+BODY_UNROLL = 32
 STAR_UNROLL = 16
 MESH = pl.DeviceIdType.MESH
 
@@ -103,9 +103,6 @@
             )
         )
     ]
-    for fetch in fetches:
-        fetch.start()
-
     barrier = pltpu.get_barrier_semaphore()
 
     def greet(w, n):
@@ -125,6 +122,9 @@
     each_wide(1, greet_peers)
     for n in beside[1:]:
         greet(wide, n)
+
+    for fetch in fetches:
+        fetch.start()
 
     lane = lax.broadcasted_iota(jnp.int32, (1, LANES), 1)
     lane4 = lax.broadcasted_iota(jnp.int32, (4, LANES), 1)
@@ -257,6 +257,8 @@
 
     some = states.at[0, pl.ds(0, n_wide - 1)]
     pltpu.make_async_copy(some, some, recv_sem).wait()
+    few = cell_in.at[pl.ds(0, n_wide - 1)]
+    pltpu.make_async_copy(few, few, cell_recv_sem).wait()
     halves = n_wide // 2
 
     def star_rows(n, i):
@@ -276,9 +278,6 @@
         return carry
 
     loop(halves, star_cols, 0)
-    few = cell_in.at[pl.ds(0, n_wide - 1)]
-    pltpu.make_async_copy(few, few, cell_recv_sem).wait()
-
     ess_start = bodies + n_wide * stars
 
     def ess_rows(e, carry):

time: 14 us -> 13.8 us (0.986)
  Pallas kernels: 13.2 us -> 13 us
    pallas_call x1, Pallas kernels: 12.6 us -> 12.4 us  [body(): pl.pallas_call(functools.partial(kernel, n_wide, n_narrow), out_shape=jax...]
where the time goes in v5:
time: 13.8 us; the launch traced here: 13.6 us
  Pallas kernels  13 us (94%)
  between operations  0.64 us (5%)
    pallas_call x1, Pallas kernels, body(): pl.pallas_call(functools.partial(kernel, n_wide, n_narrow), out_shape=jax...  12.4 us
    pallas_call x1, Pallas kernels, body(): pl.pallas_call(unpack, out_shape=(jax.ShapeDtypeStruct(gal_vel.shape, f32...  0.61 us

profile of v5, /device:TPU:0, one launch (start us, length us, event | category | flops | bytes accessed | tf_op | source)
XLA Modules:
  0.0 13.6 jit_solution(9504778887181297206)
XLA Ops:
  0.6 12.4 %shard_map.130.packed = f32[3,768]{1,0:T(4,128)S(1)} custom-call(f32[3,64]{1,0:T(4,128)} %star_pos_hbm.1, f32[3,64]{1,0:T(4,128)} %star_vel_hbm.1, f32[1,64]{1,0:T(1,128)} %bitcast.6, f32[3,64]{1,0:T(4,128)} %star_acc_hbm.1, f32[3,64]{1,0:T(4,128)} %star_jerk_hbm.1, f32[3,512]{1,0:T(4,128)} %gal_pos_hbm.1, f32[3,512]{1,0:T(4,128)} %gal_vel_hbm.1, ...), custom_call_target="tpu_custom_call" | custom-call | tf_op jit(solution)/shard_map/pallas_call | solution.py:416
  13.0 0.6 %shard_map.131 = (f32[3,512]{1,0:T(4,128)}, f32[3,64]{1,0:T(4,128)}, f32[3,64]{1,0:T(4,128)}) custom-call(f32[3,768]{1,0:T(4,128)S(1)} %shard_map.130.packed), custom_call_target="tpu_custom_call" | custom-call | tf_op jit(solution)/shard_map/pallas_call | solution.py:468
